TPU v7x, 32 devices: a whole 2x2x4 slice. The times are simulated.
32 devices in a mesh: rep: 8 (over z, x), mp: 4 (over y, core).
Axes of the slice: x: 2, y: 2, z: 4, core: 2. Of those that a mesh axis runs over, the one named last changes fastest.
Arguments:
- weight: bfloat16 [4096, 4096], P('rep', 'mp'), may hold values from -4 to 4
- tokens: bfloat16 [2048, 4096], P('rep', 'mp'), may hold values from -16 to 16
- cotangent: bfloat16 [2048, 4096], P('rep', 'mp'), may hold values from -128 to 128
- next_tokens: bfloat16 [2048, 4096], P('rep'), may hold values from -6 to 6
Outputs:
- new_weight: bfloat16 [4096, 4096], P('rep', 'mp')
- next_query: bfloat16 [2048, 4096], P('rep', 'mp')
All inputs are finite; a program needn't handle non-finite values.
Results may differ from a plain program's by a relative error of at most 0.0049.
Values may be sent and summed in bfloat16 or wider, within the bound.
A program may use at most 128 MiB of HBM per device.

v0:
```python
import jax
import jax.numpy as jnp
from jax import lax
from jax.sharding import PartitionSpec as P

learning_rate = 0.002
eps = 1e-06
HI = lax.Precision.HIGHEST


def mix(gram, replicas):
    mixing = jnp.eye(replicas, dtype=jnp.float32)
    count = replicas
    while count > 1:
        middle = count // 2
        lower = mixing[:middle]
        upper = mixing[middle:count]
        lower_gram = jnp.dot(lower, gram, precision=HI)
        upper_gram = jnp.dot(upper, gram, precision=HI)
        cross = jnp.sum(lower_gram * upper, axis=1)
        lower_sq = jnp.sum(lower_gram * lower, axis=1)
        upper_sq = jnp.sum(upper_gram * upper, axis=1)
        mixing = (1.0 - cross / (2.0 * lower_sq + eps))[:, None] * lower + (
            1.0 - cross / (2.0 * upper_sq + eps)
        )[:, None] * upper
        count = middle
    return mixing[0]


def local(weight, tokens, cotangent, next_tokens):
    replicas = lax.axis_size("rep")
    per, width = cotangent.shape
    rows = weight.shape[0]
    cots = lax.all_gather(cotangent, "rep", axis=0, tiled=False)
    own = lax.all_gather(tokens, "mp", axis=1, tiled=True)
    stacked = own.reshape(per, replicas, rows).transpose(1, 0, 2)
    toks = lax.all_to_all(stacked, "rep", split_axis=0, concat_axis=0, tiled=True)
    grads = [
        lax.dot_general(
            toks[s], cots[s], (((0,), (0,)), ((), ())), preferred_element_type=jnp.float32
        )
        for s in range(replicas)
    ]
    entries = [
        jnp.sum(grads[s] * grads[t]) for s in range(replicas) for t in range(s, replicas)
    ]
    flat = lax.psum(jnp.stack(entries), ("rep", "mp"))
    at = {}
    k = 0
    for s in range(replicas):
        for t in range(s, replicas):
            at[s, t] = at[t, s] = k
            k += 1
    gram = jnp.stack(
        [jnp.stack([flat[at[s, t]] for t in range(replicas)]) for s in range(replicas)]
    )
    coef = mix(gram, replicas)
    update = coef[0] * grads[0]
    for s in range(1, replicas):
        update = update + coef[s] * grads[s]
    new_weight = (weight.astype(jnp.float32) - learning_rate * update).astype(jnp.bfloat16)
    product = jnp.dot(
        next_tokens,
        lax.all_gather(new_weight, "rep", axis=0, tiled=True),
        preferred_element_type=jnp.float32,
    )
    features = next_tokens.shape[1]
    next_query = (product * features ** (-0.5)).astype(jnp.bfloat16)
    return (new_weight, next_query)


def solution(mesh):
    in_specs = (P("rep", "mp"), P("rep", "mp"), P("rep", "mp"), P("rep", None))
    out_specs = (P("rep", "mp"), P("rep", "mp"))
    return jax.shard_map(local, mesh=mesh, in_specs=in_specs, out_specs=out_specs, check_vma=False)
```

profile of v0, /device:TPU:0, one launch (start us, length us, event | category | flops | bytes accessed | tf_op | source)
XLA Modules:
  0.0 396.4 jit_solution(6090681871515035741)
XLA Ops:
  7.2 2.2 copy.8
  9.5 0.7 all-gather.9.cloned.1.call-update
  10.2 25.2 %all-gather.5.cloned.1.call-done = bf16[256,4096]{0,1:T(8,128)(2,1)} async-done(((bf16[256,1024]{0,1:T(8,128)(2,1)}), bf16[256,4096]{0,1:T(8,128)(2,1)}) %all-gather.5.cloned.1.call-update) | async-done | bytes 2097168 | tf_op jit(solution)/shard_map/all_gather | solution.py:35
  35.4 90.9 %all_to_all.5 = bf16[8,256,512]{1,2,0:T(8,128)(2,1)} all-to-all(bf16[8,256,512]{1,2,0:T(8,128)(2,1)} %bitcast.115), channel_id=1, replica_groups=mesh['rep'=8,'mp'=4] {'rep'}, dimensions={0} | all-to-all | bytes 4194304 | tf_op jit(solution)/shard_map/all_to_all | solution.py:37
  126.4 14.2 %all-gather.9.cloned.1.call-done = bf16[2048,1024]{1,0:T(8,128)(2,1)} async-done(((bf16[256,1024]{1,0:T(8,128)(2,1)}), bf16[2048,1024]{1,0:T(8,128)(2,1)}) %all-gather.9.cloned.1.call-update) | async-done | bytes 4194320 | tf_op jit(solution)/shard_map/all_gather | solution.py:34
  140.6 1.7 fusion.11
  142.4 2.0 fusion.13
  144.5 2.3 fusion.15
  146.8 0.4 fusion.17
  147.2 0.4 fusion.19
  147.7 0.4 fusion.7
  148.1 0.4 fusion.9
  148.7 0.7 copy-done.5
  149.5 8.4 %multiply_reduce_fusion = (f32[]{:T(128)}, f32[]{:T(128)}, f32[]{:T(128)}, f32[]{:T(128)}, f32[]{:T(128)}, /*index=5*/f32[]{:T(128)}, f32[]{:T(128)}, f32[]{:T(1...) fusion(f32[512,1024]{1,0:T(8,128)S(1)} %fusion.7, ...), kind=kOutput, calls=%fused_computation.1 | convolution fusion | flops 306184192 | bytes 17563792 | tf_op jit(solution)/shard_map/dot_general | solution.py:39
  157.9 23.2 %stack.204 = f32[36]{0:T(128)S(1)} concatenate(f32[1]{0:T(128)} %bitcast.3, f32[1]{0:T(128)} %bitcast.5, f32[1]{0:T(128)} %bitcast.7, f32[1]{0:T(128)} %bitcast.9, f32[1]{0:T(128)} %bitcast.11, f32[1]{0:T(128)} %bitcast.13, f32[1]{0:T(128)} %bitcast.15, f32[1]{0:T(128)} %bitcast.17, f32[1]{0:T(128)} %bitcast.18, f32[1]{0:T(128)} %bitcast.19, f32[1]{0:T(128)} %bitcast.20, ...), dimensions={0} | concatenate | bytes 288 | tf_op jit(solution)/shard_map/stack | solution.py:47
  181.1 36.9 %psum.7 = f32[36]{0:T(128)S(1)} all-reduce(f32[36]{0:T(128)S(1)} %stack.204), channel_id=1, replica_groups=mesh['rep'=8,'mp'=4] {'rep','mp'}, use_global_device_ids=true, to_apply=%region_36.0 | all-reduce | flops 36 | bytes 288 | tf_op jit(solution)/shard_map/psum | solution.py:47
  217.9 0.7 fusion.39
  218.8 0.7 fusion.40
  219.8 1.9 maximum_bitcast_fusion.2
  221.7 2.7 stack.212
  224.4 1.9 maximum_bitcast_fusion
  226.3 3.2 stack.214
  229.4 3.8 stack.218
  233.2 3.8 stack.216
  237.9 0.3 multiply_reduce_fusion.38
  238.3 0.7 multiply_reduce_fusion.40
  239.1 0.7 fusion.4
  242.3 0.7 fusion.37
  243.0 14.1 %subtract_convert_fusion = bf16[512,1024]{1,0:T(8,128)(2,1)} fusion(f32[512,1024]{1,0:T(8,128)} %get-tuple-element.91, f32[512,1024]{1,0:T(8,128)} %copy-done.6, f32[512,1024]{1,0:T(8,128)} %copy-done.7, f32[512,1024]{1,0:T(8,128)} %copy-done.1, f32[512,1024]{1,0:T(8,128)} %copy-done.2, f32[512,1024]{1,0:T(8,128)} %copy-done.3, f32[512,1024]{1,0:T(8,128)} %copy-done.4, ...), kind=kLoop, calls=%fused_computation | loop fusion | flops 9961472 | bytes 18874400 | tf_op jit(solution)/shard_map/convert_element_type | solution.py:61
  257.1 126.0 %all-gather.7.cloned.1.call-done = bf16[4096,1024]{1,0:T(8,128)(2,1)} async-done(((bf16[512,1024]{1,0:T(8,128)(2,1)}), bf16[4096,1024]{1,0:T(8,128)(2,1)}) %all-gather.7.cloned.1.call-update) | async-done | bytes 8388624 | tf_op jit(solution)/shard_map/all_gather | solution.py:64
  383.1 5.8 %fusion.1 = bf16[256,1024]{0,1:T(8,128)(2,1)S(1)} fusion(bf16[4096,1024]{1,0:T(8,128)(2,1)} %all-gather.7.cloned.1.call-done, bf16[256,4096]{1,0:T(8,128)(2,1)S(1)} %copy-done), kind=kOutput, calls=%fused_computation.39 | convolution fusion | flops 2148007936 | bytes 11010048 | tf_op jit(solution)/shard_map/dot_general | solution.py:62
  388.9 1.0 copy.17
  (42 shorter events, 1.8 us)
Async XLA Ops:
  7.2 375.9 %copy-start = (bf16[256,4096]{1,0:T(8,128)(2,1)S(1)}, bf16[256,4096]{1,0:T(8,128)(2,1)}, u32[]{:S(2)}) copy-start(bf16[256,4096]{1,0:T(8,128)(2,1)} %param.7) | copy-start | bytes 6291460
  7.2 28.3 %all-gather.5.cloned.1.call-start = ((), (), s32[]{:S(2)}) async-start(), calls=%async_computation.1 | async-start | bytes 2621440 | tf_op jit(solution)/shard_map/all_gather | solution.py:35
  9.4 131.2 %all-gather.9.cloned.1.call-start = ((), (), s32[]{:S(2)}) async-start(), calls=%async_computation.3 | async-start | bytes 4718592 | tf_op jit(solution)/shard_map/all_gather | solution.py:34
  10.2 372.9 %all-gather.7.cloned.1.call-start = ((), (), s32[]{:S(2)}) async-start(), calls=%async_computation.2 | async-start | bytes 9437184 | tf_op jit(solution)/shard_map/all_gather | solution.py:64
  140.6 1.8 copy-start.8
  142.4 6.2 %copy-start.1 = (f32[512,1024]{1,0:T(8,128)}, f32[512,1024]{1,0:T(8,128)S(1)}, u32[]{:S(2)}) copy-start(f32[512,1024]{1,0:T(8,128)S(1)} %fusion.11) | copy-start | bytes 6291460
  142.4 4.3 %copy-start.9 = (bf16[2048,1024]{1,0:T(8,128)(2,1)S(1)}, bf16[2048,1024]{1,0:T(8,128)(2,1)}, u32[]{:S(2)}) copy-start(bf16[2048,1024]{1,0:T(8,128)(2,1)} %all-gather.9.cloned.1.call-done) | copy-start | bytes 12582916
  144.5 4.1 %copy-start.2 = (f32[512,1024]{1,0:T(8,128)}, f32[512,1024]{1,0:T(8,128)S(1)}, u32[]{:S(2)}) copy-start(f32[512,1024]{1,0:T(8,128)S(1)} %fusion.13) | copy-start | bytes 6291460
  146.8 1.8 copy-start.3
  147.2 1.5 copy-start.4
  147.7 1.8 copy-start.5
  148.1 9.7 %copy-start.6 = (f32[512,1024]{1,0:T(8,128)}, f32[512,1024]{1,0:T(8,128)S(1)}, u32[]{:S(2)}) copy-start(f32[512,1024]{1,0:T(8,128)S(1)} %fusion.7) | copy-start | bytes 6291460
  149.5 8.4 %copy-start.7 = (f32[512,1024]{1,0:T(8,128)}, f32[512,1024]{1,0:T(8,128)S(1)}, u32[]{:S(2)}) copy-start(f32[512,1024]{1,0:T(8,128)S(1)} %fusion.9) | copy-start | bytes 6291460
  149.5 93.5 %copy-start.10 = (bf16[512,1024]{1,0:T(8,128)(2,1)S(1)}, bf16[512,1024]{1,0:T(8,128)(2,1)}, u32[]{:S(2)}) copy-start(bf16[512,1024]{1,0:T(8,128)(2,1)} %param.4) | copy-start | bytes 3145732
Sparse Core Ops, SparseCore 0:
  10.1 25.2 all-gather.4
  37.6 102.9 all-gather.8
  257.2 125.8 all-gather.6
where the time goes:
time: 397 us; the launch traced here: 396 us
  waiting for transfers between devices  166 us (42%)
  blocking collectives  128 us (32%)
  local copies, waits for them, and re-layouts  43.4 us (11%)
  matrix products  24.5 us (6%)
  other arithmetic  18.1 us (5%)
  between operations  16.4 us (4%)
    all_gather x1, waiting for transfers between devices, local(): lax.all_gather(new_weight, 'rep', axis=0, tiled=True)  126 us
    all_to_all x1, blocking collectives, local(): lax.all_to_all(stacked, 'rep', split_axis=0, concat_axis=0, tiled=True)  90.9 us
    psum x1, blocking collectives, local(): flat = lax.psum(jnp.stack(entries), ('rep', 'mp'))  36.9 us
    all_gather x1, waiting for transfers between devices, local(): own = lax.all_gather(tokens, 'mp', axis=1, tiled=True)  25.2 us
    another operation x1, local copies, waits for them, and re-layouts, local(): flat = lax.psum(jnp.stack(entries), ('rep', 'mp'))  23.2 us
    dot_general x8, matrix products, local(): lax.dot_general(toks[s], cots[s], (((0,), (0,)), ((), ())), preferred_ele...  16.2 us
    all_gather x1, waiting for transfers between devices, local(): cots = lax.all_gather(cotangent, 'rep', axis=0, tiled=False)  14.2 us
    convert_element_type x1, other arithmetic, local(): (weight.astype(jnp.float32) - learning_rate * update).astype(jnp.bfloat16)  14.1 us
  transfers between devices with their start and end apart: 3, of which 3 were waited for; matrix products, arithmetic and copies ran while one was open for 0% of the time, Pallas kernels for 0%

commit v1 on v0

v1 whole, which is shorter than its diff:
```python
import functools

import jax
import jax.numpy as jnp
from jax import lax
from jax.experimental import pallas as pl
from jax.experimental.pallas import tpu as pltpu
from jax.sharding import PartitionSpec as P

learning_rate = 0.002
eps = 1e-06
F32 = jnp.float32
BF16 = jnp.bfloat16
MESH = pl.DeviceIdType.MESH
LANES = 128


def x_size(replicas):
    x = 1
    while 2 * (2 * x) ** 2 <= replicas and replicas % (2 * x) == 0:
        x *= 2
    return x


def aligned(start, size):
    return pl.ds(pl.multiple_of(start * size, size), size)


def kernel(
    sizes,
    w_hbm,
    t_hbm,
    c_hbm,
    n_hbm,
    wo_hbm,
    q_hbm,
    cbuf,
    t1buf,
    tfull,
    ttr,
    nbuf,
    grads,
    gloc,
    gmp,
    grep,
    wown,
    wbuf,
    part,
    rsend,
    rrecv,
    qbuf,
    local_sem,
    c_own,
    c_fwd,
    c_xs,
    c_rs,
    t1_s,
    t1_r,
    t2_s,
    t2_r,
    t3_s,
    t3_r,
    n2_s,
    n2_r,
    n3_s,
    n3_r,
    gm_s,
    gm_r,
    gr_s,
    gr_r,
    w_s,
    w_r,
    rs_s,
    rs_r,
):
    Z, X, M, width = sizes
    R = Z * X
    _, tok, cols = cbuf.shape
    rows = tfull.shape[2]
    feats = X * rows
    per = cols // rows
    tq = tok // M
    ntok = nbuf.shape[1]
    nq = ntok // M
    blocks = cols // width
    group = min(8, R)
    grows = gloc.shape[0]

    me = lax.axis_index("rep")
    m = lax.axis_index("mp")
    z = me // X
    x = lax.rem(me, X)

    def nearest(j):
        found = jnp.int32(0)
        for a in range(Z):
            order = sorted(range(Z), key=lambda b: (abs(b - a), b))
            for i in range(Z):
                found = found + jnp.where((z == a) & (j == i), order[i], 0)
        return found

    def remote(src, dst, send, recv, r, mm):
        return pltpu.make_async_remote_copy(
            src_ref=src,
            dst_ref=dst,
            send_sem=send,
            recv_sem=recv,
            device_id=(r, mm),
            device_id_type=MESH,
        )

    def other_x(o):
        return lax.rem(x + o, X)

    def other_m(o):
        return lax.rem(m + o, M)

    def other_r(o):
        return lax.rem(me + o, R)

    def at(zz, xx):
        return zz * X + xx

    def own_copies():
        return [
            pltpu.make_async_copy(c_hbm, cbuf.at[me], local_sem.at[0]),
            pltpu.make_async_copy(t_hbm.at[aligned(m, tq), :], t1buf.at[m], local_sem.at[1]),
            pltpu.make_async_copy(n_hbm.at[:, aligned(z, feats)], nbuf.at[z], local_sem.at[2]),
            pltpu.make_async_copy(w_hbm, wown, local_sem.at[3]),
        ]

    for copy in own_copies():
        copy.start()

    barrier = pltpu.get_barrier_semaphore()
    for o in range(1, M):
        pl.semaphore_signal(barrier, inc=1, device_id=(me, other_m(o)), device_id_type=MESH)
    for o in range(1, R):
        pl.semaphore_signal(barrier, inc=1, device_id=(other_r(o), m), device_id_type=MESH)
    pl.semaphore_wait(barrier, M + R - 2)

    def t1(o):
        mm = other_m(o)
        return remote(t_hbm.at[aligned(mm, tq), :], t1buf.at[m], t1_s.at[o], t1_r.at[o], me, mm)

    for o in range(1, M):
        t1(o).start()

    def c_up():
        return remote(c_hbm, cbuf.at[me], c_own.at[0], c_rs.at[me], at(z + 1, x), m)

    def c_down():
        return remote(c_hbm, cbuf.at[me], c_own.at[1], c_rs.at[me], at(z - 1, x), m)

    def c_across(j, o):
        r = at(nearest(j), x)
        return remote(cbuf.at[r], cbuf.at[r], c_xs.at[j, o], c_rs.at[r], at(z, other_x(o)), m)

    def c_forward(j):
        zz = nearest(j)
        r = at(zz, x)
        to = jnp.where(zz < z, z + 1, z - 1)
        return (
            (to >= 0) & (to < Z),
            lambda: remote(cbuf.at[r], cbuf.at[r], c_fwd.at[j], c_rs.at[r], at(to, x), m),
        )

    pl.when(z < Z - 1)(lambda: c_up().start())
    pl.when(z > 0)(lambda: c_down().start())
    own = own_copies()
    own[0].wait()
    for o in range(1, X):
        c_across(0, o).start()

    def zero(i, carry):
        for r in range(R):
            grads[r, aligned(i, 8), :] = jnp.zeros((8, cols), F32)
        return carry

    lax.fori_loop(0, rows // 8, zero, 0)
    gloc[...] = jnp.zeros_like(gloc)

    own[1].wait()
    for o in range(1, M):
        t1(o).wait_recv()

    def t2_src(r):
        return t1buf.at[r // per, :, aligned(lax.rem(r, per), rows)]

    def t2(o):
        r = other_r(o)
        return remote(t2_src(r), tfull.at[me, aligned(m, tq), :], t2_s.at[o], t2_r.at[me], r, m)

    for o in range(1, R):
        t2(o).start()
    mine = pltpu.make_async_copy(t2_src(me), tfull.at[me, aligned(m, tq), :], local_sem.at[4])
    mine.start()
    mine.wait()

    def t3(r, o):
        piece = tfull.at[r, aligned(m, tq), :]
        return remote(piece, piece, t3_s.at[r], t3_r.at[r], me, other_m(o))

    def t3_start(r):
        for o in range(1, M):
            t3(r, o).start()

    def wait_all(buffer, sem):
        pltpu.make_async_copy(buffer, buffer, sem).wait()

    def t3_wait(r, sem):
        wait_all(tfull.at[r, pl.ds(0, (M - 1) * tq), :], sem.at[r])

    def t2_wait(r):
        piece = tfull.at[r, aligned(m, tq), :]
        pltpu.make_async_copy(piece, piece, t2_r.at[r]).wait()

    t3_start(me)
    for o in range(1, X):
        r = at(z, other_x(o))
        t2_wait(r)
        t3_start(r)

    def n2(o):
        zz = lax.rem(z + o, Z)
        return remote(
            n_hbm.at[aligned(m, nq), aligned(zz, feats)],
            nbuf.at[z, aligned(m, nq), :],
            n2_s.at[o],
            n2_r.at[z],
            at(zz, x),
            m,
        )

    def n3(zz, o):
        piece = nbuf.at[zz, aligned(m, nq), :]
        return remote(piece, piece, n3_s.at[zz], n3_r.at[zz], me, other_m(o))

    def n2_start():
        for o in range(1, Z):
            n2(o).start()

    def n3_start():
        for o in range(1, Z):
            zz = lax.rem(z + o, Z)
            piece = nbuf.at[zz, aligned(m, nq), :]
            pltpu.make_async_copy(piece, piece, n2_r.at[zz]).wait()
            for p in range(1, M):
                n3(zz, p).start()

    def process(r):
        ttr[...] = tfull[r].T
        tile = min(256, cols)

        def grad_tile(i, carry):
            at_cols = aligned(i, tile)
            grads[r, :, at_cols] = jnp.dot(
                ttr[...], cbuf[r, :, at_cols], preferred_element_type=F32
            )
            return carry

        lax.fori_loop(0, cols // tile, grad_tile, 0)
        sub = lax.broadcasted_iota(jnp.int32, gloc.shape, 0)
        lane = lax.broadcasted_iota(jnp.int32, gloc.shape, 1)

        def dots(g, carry):
            def row(i, sums):
                new = grads[r, aligned(i, 8), :]
                out = []
                for q in range(group):
                    prod = new * grads[g * group + q, aligned(i, 8), :]
                    total = sums[q]
                    for a in range(cols // LANES):
                        total = total + prod[:, a * LANES : (a + 1) * LANES]
                    out.append(total)
                return tuple(out)

            sums = lax.fori_loop(
                0, rows // 8, row, tuple(jnp.zeros((8, LANES), F32) for _ in range(group))
            )
            gram = gloc[...]
            for q in range(group):
                other = g * group + q
                total = jnp.sum(jnp.sum(sums[q], axis=1, keepdims=True), axis=0, keepdims=True)
                here = ((sub == r) & (lane == other)) | ((sub == other) & (lane == r))
                gram = gram + jnp.where(here, total, 0.0)
            gloc[...] = gram
            return carry

        lax.fori_loop(0, R // group, dots, 0)

    def step(j, carry):
        zz = nearest(j)

        @pl.when((j >= 1) & (j < Z))
        def _():
            r = at(zz, x)
            pltpu.make_async_copy(cbuf.at[r], cbuf.at[r], c_rs.at[r]).wait()
            ok, copy = c_forward(j)
            pl.when(ok)(lambda: copy().start())
            for o in range(1, X):
                c_across(j, o).start()

        @pl.when(j < Z - 1)
        def _():
            ahead = nearest(j + 1)
            for o in range(X):
                r = at(ahead, other_x(o))
                t2_wait(r)
                t3_start(r)

        pl.when(j == Z - 2)(n2_start)
        pl.when(j == Z - 1)(n3_start)

        @pl.when(j < Z)
        def _():
            r = at(zz, x)
            t3_wait(r, t3_r)
            process(r)

        @pl.when(j >= 1)
        def _():
            for o in range(1, X):
                r = at(nearest(j - 1), other_x(o))
                pltpu.make_async_copy(cbuf.at[r], cbuf.at[r], c_rs.at[r]).wait()
                t3_wait(r, t3_r)
                process(r)

        return carry

    lax.fori_loop(0, Z + 1, step, 0)

    def gm(o):
        return remote(gmp.at[m], gmp.at[m], gm_s.at[o], gm_r.at[o], me, other_m(o))

    def gr(o):
        return remote(grep.at[me], grep.at[me], gr_s.at[o], gr_r.at[o], other_r(o), m)

    gmp[m] = gloc[...]
    for o in range(1, M):
        gm(o).start()
    for o in range(1, M):
        gm(o).wait_recv()
    total = gmp[0]
    for o in range(1, M):
        total = total + gmp[o]
    grep[me] = total
    for o in range(1, R):
        gr(o).start()
    for o in range(1, R):
        gr(o).wait_recv()
    gram = grep[0]
    for o in range(1, R):
        gram = gram + grep[o]

    sub = lax.broadcasted_iota(jnp.int32, (grows, LANES), 0)
    lane = lax.broadcasted_iota(jnp.int32, (grows, LANES), 1)
    lane1 = lax.broadcasted_iota(jnp.int32, (1, LANES), 1)
    coef = jnp.ones((1, LANES), F32)
    count = R
    while count > 1:
        half = count // 2
        inside = (sub < count) & (lane < count)
        gram = jnp.where(inside, gram, 0.0)
        diagonal = jnp.where(sub == lane, gram, 0.0)
        crossed = jnp.where((sub == lane + half) | (lane == sub + half), gram, 0.0)
        factors = []
        for axis in (0, 1):
            square = jnp.sum(diagonal, axis=axis, keepdims=True)
            cross = jnp.sum(crossed, axis=axis, keepdims=True)
            factors.append(1.0 - cross / (2.0 * square + eps))
        scaled = jnp.where(inside, factors[0] * gram * factors[1], 0.0)
        scaled = scaled + pltpu.roll(scaled, LANES - half, 1)
        gram = scaled + pltpu.roll(scaled, grows - half, 0)
        along = jnp.broadcast_to(jnp.where(lane1 < count, factors[0], 0.0), (8, LANES))
        reach = count
        while reach < R:
            along = along + pltpu.roll(along, reach, 1)
            reach *= 2
        coef = coef * along[:1]
        count = half
    weights = [
        jnp.sum(jnp.where(lane1 == r, coef, 0.0), axis=1, keepdims=True) for r in range(R)
    ]

    own[3].wait()
    tall = 16

    def w_rows(xx):
        return aligned(xx, rows)

    def w_across(b, o):
        piece = wbuf.at[w_rows(x), aligned(b, width)]
        return remote(piece, piece, w_s.at[b, o], w_r.at[b, x], at(z, other_x(o)), m)

    def update(b, carry):
        at_cols = aligned(b, width)

        def row(i, inner):
            at_rows = aligned(i, tall)
            total = weights[0] * grads[0, at_rows, at_cols]
            for r in range(1, R):
                total = total + weights[r] * grads[r, at_rows, at_cols]
            new = wown[at_rows, at_cols].astype(F32) - learning_rate * total
            wbuf[pl.ds(pl.multiple_of(x * rows + i * tall, tall), tall), at_cols] = new.astype(
                BF16
            )
            return inner

        lax.fori_loop(0, rows // tall, row, 0)
        for o in range(1, X):
            w_across(b, o).start()
        return carry

    lax.fori_loop(0, blocks, update, 0)
    w_out = pltpu.make_async_copy(wbuf.at[w_rows(x), :], wo_hbm, local_sem.at[5])
    w_out.start()

    own[2].wait()
    for o in range(1, Z):
        zz = lax.rem(z + o, Z)
        wait_all(nbuf.at[zz, pl.ds(0, (M - 1) * nq), :], n3_r.at[zz])

    def r_send(dest, b):
        to = jnp.where(dest > z, z + 1, z - 1)
        slot = jnp.where((to == dest) & (dest < z), Z, dest)
        at_cols = aligned(b, width)
        return remote(
            rsend.at[dest, :, at_cols],
            rrecv.at[slot, :, at_cols],
            rs_s.at[dest, b],
            rs_r.at[slot, b],
            at(to, x),
            m,
        )

    def r_wait(slot, b):
        piece = rrecv.at[slot, :, aligned(b, width)]
        pltpu.make_async_copy(piece, piece, rs_r.at[slot, b]).wait()

    scale = cols * M

    def product(b, carry):
        at_cols = aligned(b, width)
        for o in range(1, X):
            xx = other_x(o)
            piece = wbuf.at[w_rows(xx), at_cols]
            pltpu.make_async_copy(piece, piece, w_r.at[b, xx]).wait()

        def one(dest, inner):
            part[dest] = jnp.dot(nbuf[dest], wbuf[:, at_cols], preferred_element_type=F32)
            return inner

        lax.fori_loop(0, Z, one, 0)
        for i in range(Z - 1, 0, -1):
            dest = nearest(i)
            before = jnp.where(dest > z, z - 1, z + 1)
            more = (before >= 0) & (before < Z)

            @pl.when(more)
            def _():
                r_wait(dest, b)
                rsend[dest, :, at_cols] = (
                    part[dest] + rrecv[dest, :, at_cols].astype(F32)
                ).astype(BF16)

            @pl.when(jnp.logical_not(more))
            def _():
                rsend[dest, :, at_cols] = part[dest].astype(BF16)

            r_send(dest, b).start()

        @pl.when(z > 0)
        def _():
            r_wait(z, b)
            part[z] = part[z] + rrecv[z, :, at_cols].astype(F32)

        @pl.when(z < Z - 1)
        def _():
            r_wait(Z, b)
            part[z] = part[z] + rrecv[Z, :, at_cols].astype(F32)

        qbuf[:, at_cols] = (part[z] * scale**-0.5).astype(BF16)
        return carry

    lax.fori_loop(0, blocks, product, 0)
    q_out = pltpu.make_async_copy(qbuf, q_hbm, local_sem.at[6])
    q_out.start()

    pl.when(z < Z - 1)(lambda: c_up().wait_send())
    pl.when(z > 0)(lambda: c_down().wait_send())
    for o in range(1, X):
        for j in range(Z):
            c_across(j, o).wait_send()
    for j in range(1, Z):
        ok, copy = c_forward(j)
        pl.when(ok)(lambda copy=copy: copy().wait_send())
    for o in range(1, M):
        t1(o).wait_send()
        gm(o).wait_send()
    for o in range(1, R):
        t2(o).wait_send()
        gr(o).wait_send()
    for r in range(R):
        t3_wait(r, t3_s)
    for o in range(1, Z):
        n2(o).wait_send()
        zz = lax.rem(z + o, Z)
        wait_all(nbuf.at[zz, pl.ds(0, (M - 1) * nq), :], n3_s.at[zz])
    for b in range(blocks):
        for o in range(1, X):
            w_across(b, o).wait_send()
        for i in range(1, Z):
            r_send(nearest(i), b).wait_send()
    w_out.wait()
    q_out.wait()


def local(weight, tokens, cotangent, next_tokens):
    R = lax.axis_size("rep")
    M = lax.axis_size("mp")
    X = x_size(R)
    Z = R // X
    tok, cols = cotangent.shape
    rows = weight.shape[0]
    ntok = next_tokens.shape[0]
    width = min(256, cols)
    blocks = cols // width
    grows = max(8, R)
    dma = pltpu.SemaphoreType.DMA
    anywhere = pl.BlockSpec(memory_space=pl.ANY)
    return pl.pallas_call(
        functools.partial(kernel, (Z, X, M, width)),
        out_shape=(
            jax.ShapeDtypeStruct((rows, cols), BF16),
            jax.ShapeDtypeStruct((ntok, cols), BF16),
        ),
        in_specs=[anywhere] * 4,
        out_specs=(anywhere, anywhere),
        scratch_shapes=[
            pltpu.VMEM((R, tok, cols), BF16),
            pltpu.VMEM((M, tok // M, cols), BF16),
            pltpu.VMEM((R, tok, rows), BF16),
            pltpu.VMEM((rows, tok), BF16),
            pltpu.VMEM((Z, ntok, X * rows), BF16),
            pltpu.VMEM((R, rows, cols), F32),
            pltpu.VMEM((grows, LANES), F32),
            pltpu.VMEM((M, grows, LANES), F32),
            pltpu.VMEM((R, grows, LANES), F32),
            pltpu.VMEM((rows, cols), BF16),
            pltpu.VMEM((X * rows, cols), BF16),
            pltpu.VMEM((Z, ntok, width), F32),
            pltpu.VMEM((Z, ntok, cols), BF16),
            pltpu.VMEM((Z + 1, ntok, cols), BF16),
            pltpu.VMEM((ntok, cols), BF16),
            dma((7,)),
            dma((2,)),
            dma((Z,)),
            dma((Z, X)),
            dma((R,)),
            dma((M,)),
            dma((M,)),
            dma((R,)),
            dma((R,)),
            dma((R,)),
            dma((R,)),
            dma((Z,)),
            dma((Z,)),
            dma((Z,)),
            dma((Z,)),
            dma((M,)),
            dma((M,)),
            dma((R,)),
            dma((R,)),
            dma((blocks, X)),
            dma((blocks, X)),
            dma((Z, blocks)),
            dma((Z + 1, blocks)),
        ],
        compiler_params=pltpu.CompilerParams(
            collective_id=0, has_side_effects=True, vmem_limit_bytes=60 * 1024 * 1024
        ),
    )(weight, tokens, cotangent, next_tokens)


def solution(mesh):
    in_specs = (P("rep", "mp"), P("rep", "mp"), P("rep", "mp"), P("rep", None))
    out_specs = (P("rep", "mp"), P("rep", "mp"))
    return jax.shard_map(local, mesh=mesh, in_specs=in_specs, out_specs=out_specs, check_vma=False)
```

time: 397 us -> 161 us (0.41)
  waiting for transfers between devices: 166 us -> 0 us
  Pallas kernels: 0 us -> 157 us
  blocking collectives: 128 us -> 0 us
  local copies, waits for them, and re-layouts: 43.4 us -> 3.12 us
  matrix products: 24.5 us -> 0 us
  other arithmetic: 18.1 us -> 0 us
  between operations: 16.4 us -> 0.65 us
    all_gather x3 -> x0, waiting for transfers between devices: 165 us -> none  [the longest x1 126 us: local(): lax.all_gather(new_weight, 'rep', axis=0, tiled=True)]
    pallas_call x0 -> x1, Pallas kernels: none -> 157 us  [local(): pl.pallas_call(functools.partial(kernel, (Z, X, M, width)), out_shape=(ja...]
    all_to_all x1 -> x0, blocking collectives: 90.9 us -> none  [local(): lax.all_to_all(stacked, 'rep', split_axis=0, concat_axis=0, tiled=True)]
    psum x1 -> x0, blocking collectives: 36.9 us -> none  [local(): flat = lax.psum(jnp.stack(entries), ('rep', 'mp'))]
    another operation x6 -> x0, local copies, waits for them, and re-layouts: 36.6 us -> none  [the longest x1 23.2 us: local(): flat = lax.psum(jnp.stack(entries), ('rep', 'mp'))]
    dot_general x15 -> x0, matrix products: 24.5 us -> none  [the longest x8 16.2 us: local(): lax.dot_general(toks[s], cots[s], (((0,), (0,)), ((), ())), preferred_ele...]
    convert_element_type x1 -> x0, other arithmetic: 14.1 us -> none  [local(): (weight.astype(jnp.float32) - learning_rate * update).astype(jnp.bfloat16)]
  transfers between devices with their start and end apart: 3 -> 0, of which waited for: 3 -> 0; matrix products, arithmetic and copies ran while one was open for 0% -> 0% of each run, Pallas kernels for 0% -> 0%
where the time goes in v1:
time: 161 us
  Pallas kernels  157 us (98%)
  local copies, waits for them, and re-layouts  3.12 us (2%)
    pallas_call x1, Pallas kernels, local(): pl.pallas_call(functools.partial(kernel, (Z, X, M, width)), out_shape=(ja...  157 us

profile of v1, /device:TPU:0, one launch (start us, length us, event | category | flops | bytes accessed | tf_op | source)
XLA Modules:
  0.0 160.9 jit_solution(5842406998595256944)
XLA Ops:
  0.6 157.1 %shard_map.59 = (bf16[512,1024]{1,0:T(8,128)(2,1)}, bf16[256,1024]{1,0:T(8,128)(2,1)}) custom-call(bf16[512,1024]{1,0:T(8,128)(2,1)} %w_hbm.1, bf16[256,1024]{1,0:T(8,128)(2,1)} %t_hbm.1, bf16[256,1024]{1,0:T(8,128)(2,1)} %c_hbm.1, bf16[256,4096]{1,0:T(8,128)(2,1)} %n_hbm.1), custom_call_target="tpu_custom_call" | custom-call | tf_op jit(solution)/shard_map/pallas_call | solution.py:532
  157.8 0.0 copy-start
  157.8 2.3 %copy.8 = bf16[512,1024]{1,0:T(8,128)(2,1)} copy(bf16[512,1024]{1,0:T(8,128)(2,1)} %get-tuple-element.4) | data formatting | bytes 2097152
  160.1 0.0 copy-done
  160.1 0.8 copy.9
Async XLA Ops:
  157.8 2.3 %copy-start = (bf16[256,1024]{1,0:T(8,128)(2,1)S(1)}, bf16[256,1024]{1,0:T(8,128)(2,1)}, u32[]{:S(2)}) copy-start(bf16[256,1024]{1,0:T(8,128)(2,1)} %get-tuple-element.5) | copy-start | bytes 1572868

commit v2 on v1

v2 whole, which is shorter than its diff:
```python
import functools

import jax
import jax.numpy as jnp
from jax import lax
from jax.experimental import pallas as pl
from jax.experimental.pallas import tpu as pltpu
from jax.sharding import PartitionSpec as P

learning_rate = 0.002
eps = 1e-06
F32 = jnp.float32
BF16 = jnp.bfloat16
MESH = pl.DeviceIdType.MESH
LANES = 128


def x_size(replicas):
    x = 1
    while 2 * (2 * x) ** 2 <= replicas and replicas % (2 * x) == 0:
        x *= 2
    return x


def aligned(start, size):
    return pl.ds(pl.multiple_of(start * size, size), size)


def kernel(
    sizes,
    w_hbm,
    t_hbm,
    c_hbm,
    n_hbm,
    wo_hbm,
    q_hbm,
    cbuf,
    t1buf,
    tfull,
    ttr,
    nbuf,
    grads,
    gloc,
    gmp,
    grep,
    wown,
    wbuf,
    part,
    qsum,
    rsend,
    rrecv,
    qbuf,
    local_sem,
    c_own,
    c_fwd,
    c_xs,
    c_rs,
    t1_s,
    t1_r,
    t2_s,
    t2_r,
    t3_s,
    t3_r,
    n2_s,
    n2_r,
    n3_s,
    n3_r,
    gm_s,
    gm_r,
    gr_s,
    gr_r,
    w_s,
    w_r,
    rs_s,
    rs_r,
):
    Z, X, M, width = sizes
    R = Z * X
    _, parts, tok, piece_cols = cbuf.shape
    cols = parts * piece_cols
    rows = tfull.shape[2]
    feats = X * rows
    tq = tok // M
    ntok = nbuf.shape[1]
    nq = ntok // M
    blocks = cols // width
    group = min(8, R)
    grows = gloc.shape[0]

    me = lax.axis_index("rep")
    m = lax.axis_index("mp")
    z = me // X
    x = lax.rem(me, X)

    def nearest(j):
        found = jnp.int32(0)
        for a in range(Z):
            order = sorted(range(Z), key=lambda b: (abs(b - a), b))
            for i in range(Z):
                found = found + jnp.where((z == a) & (j == i), order[i], 0)
        return found

    def remote(src, dst, send, recv, r, mm):
        return pltpu.make_async_remote_copy(
            src_ref=src,
            dst_ref=dst,
            send_sem=send,
            recv_sem=recv,
            device_id=(r, mm),
            device_id_type=MESH,
        )

    def arrived(piece, sem):
        pltpu.make_async_copy(piece, piece, sem).wait()

    def other_x(o):
        return lax.rem(x + o, X)

    def other_m(o):
        return lax.rem(m + o, M)

    def other_r(o):
        return lax.rem(me + o, R)

    def at(zz, xx):
        return zz * X + xx

    def c_mine(h):
        return c_hbm.at[:, aligned(h, piece_cols)]

    def own_copies():
        copies = [
            pltpu.make_async_copy(c_mine(h), cbuf.at[me, h], local_sem.at[5 + h])
            for h in range(parts)
        ]
        own_tokens = t1buf.at[:, aligned(m, cols)]
        return [
            pltpu.make_async_copy(n_hbm.at[:, aligned(z, feats)], nbuf.at[z], local_sem.at[0]),
            pltpu.make_async_copy(w_hbm, wown, local_sem.at[1]),
            pltpu.make_async_copy(t_hbm.at[aligned(m, tq), :], own_tokens, local_sem.at[2]),
        ] + copies

    for copy in own_copies():
        copy.start()

    barrier = pltpu.get_barrier_semaphore()
    for o in range(1, M):
        pl.semaphore_signal(barrier, inc=1, device_id=(me, other_m(o)), device_id_type=MESH)
    for o in range(1, R):
        pl.semaphore_signal(barrier, inc=1, device_id=(other_r(o), m), device_id_type=MESH)
    pl.semaphore_wait(barrier, M + R - 2)

    def t1(o):
        mm = other_m(o)
        return remote(
            t_hbm.at[aligned(mm, tq), :],
            t1buf.at[:, aligned(m, cols)],
            t1_s.at[o],
            t1_r.at[o],
            me,
            mm,
        )

    for o in range(1, M):
        t1(o).start()

    def c_up(h):
        return remote(
            c_mine(h), cbuf.at[me, h], c_own.at[0, h], c_rs.at[me, h], at(z + 1, x), m
        )

    def c_down(h):
        return remote(
            c_mine(h), cbuf.at[me, h], c_own.at[1, h], c_rs.at[me, h], at(z - 1, x), m
        )

    def c_across(j, h, o):
        r = at(nearest(j), x)
        here = cbuf.at[r, h]
        return remote(here, here, c_xs.at[j, h, o], c_rs.at[r, h], at(z, other_x(o)), m)

    def c_forward(j, h):
        zz = nearest(j)
        r = at(zz, x)
        to = jnp.where(zz < z, z + 1, z - 1)
        here = cbuf.at[r, h]
        return (
            (to >= 0) & (to < Z),
            lambda: remote(here, here, c_fwd.at[j, h], c_rs.at[r, h], at(to, x), m),
        )

    own = own_copies()
    for h in range(parts):
        pl.when(z < Z - 1)(lambda h=h: c_up(h).start())
        pl.when(z > 0)(lambda h=h: c_down(h).start())
        own[3 + h].wait()
        for o in range(1, X):
            c_across(0, h, o).start()

    def zero(i, carry):
        for r in range(R):
            grads[r, aligned(i, 8), :] = jnp.zeros((8, cols), F32)
        return carry

    lax.fori_loop(0, rows // 8, zero, 0)
    gloc[...] = jnp.zeros_like(gloc)

    own[2].wait()
    for o in range(1, M):
        t1(o).wait_recv()

    def t2(j, o):
        r = at(nearest(j), other_x(o))
        return remote(
            t1buf.at[:, aligned(r, rows)],
            tfull.at[me, aligned(m, tq), :],
            t2_s.at[j * X + o],
            t2_r.at[me],
            r,
            m,
        )

    mine = tfull.at[me, aligned(m, tq), :]
    pltpu.make_async_copy(t1buf.at[:, aligned(me, rows)], mine, t2_r.at[me]).start()
    for j in range(Z):
        for o in range(1 if j == 0 else 0, X):
            t2(j, o).start()

    def t3(r, o):
        here = tfull.at[r, aligned(m, tq), :]
        return remote(here, here, t3_s.at[r], t3_r.at[r], me, other_m(o))

    def t3_start(j):
        for xo in range(X):
            r = at(nearest(j), other_x(xo))
            arrived(tfull.at[r, aligned(m, tq), :], t2_r.at[r])
            for o in range(1, M):
                t3(r, o).start()

    def t3_wait(r, sem):
        arrived(tfull.at[r, pl.ds(0, (M - 1) * tq), :], sem.at[r])

    def pass_cotangent(j):
        r = at(nearest(j), x)
        for h in range(parts):
            arrived(cbuf.at[r, h], c_rs.at[r, h])
            ok, copy = c_forward(j, h)
            pl.when(ok)(lambda copy=copy: copy().start())
            for o in range(1, X):
                c_across(j, h, o).start()

    lead = min(2, Z)
    for j in range(lead):
        if j > 0:
            pass_cotangent(j)
        t3_start(j)

    def n2(i):
        zz = nearest(i)
        return remote(
            n_hbm.at[aligned(m, nq), aligned(zz, feats)],
            nbuf.at[z, aligned(m, nq), :],
            n2_s.at[i],
            n2_r.at[z],
            at(zz, x),
            m,
        )

    def n3(zz, o):
        here = nbuf.at[zz, aligned(m, nq), :]
        return remote(here, here, n3_s.at[zz], n3_r.at[zz], me, other_m(o))

    def n2_start():
        for i in range(Z - 1, 0, -1):
            n2(i).start()

    def n3_start(i):
        zz = nearest(i)
        here = nbuf.at[zz, aligned(m, nq), :]
        arrived(here, n2_r.at[zz])
        for p in range(1, M):
            n3(zz, p).start()

    def n3_wait(zz, sem):
        arrived(nbuf.at[zz, pl.ds(0, (M - 1) * nq), :], sem.at[zz])

    def turn(r):
        t3_wait(r, t3_r)
        ttr[r] = tfull[r].T

    def process(r, h):
        tile = min(256, piece_cols)

        def grad_tile(i, carry):
            at_cols = pl.ds(pl.multiple_of(h * piece_cols + i * tile, tile), tile)
            grads[r, :, at_cols] = jnp.dot(
                ttr[r], cbuf[r, h, :, aligned(i, tile)], preferred_element_type=F32
            )
            return carry

        lax.fori_loop(0, piece_cols // tile, grad_tile, 0)
        high = min(32, rows)
        sub = lax.broadcasted_iota(jnp.int32, gloc.shape, 0)
        lane = lax.broadcasted_iota(jnp.int32, gloc.shape, 1)

        def dots(g, carry):
            def row(i, sums):
                at_rows = aligned(i, high)
                at_cols = aligned(h, piece_cols)
                new = grads[r, at_rows, at_cols]
                out = []
                for q in range(group):
                    prod = new * grads[g * group + q, at_rows, at_cols]
                    terms = [
                        prod[k * 8 : k * 8 + 8, a * LANES : (a + 1) * LANES]
                        for k in range(high // 8)
                        for a in range(piece_cols // LANES)
                    ]
                    while len(terms) > 1:
                        terms = [
                            sum(terms[k + 1 : k + 2], terms[k]) for k in range(0, len(terms), 2)
                        ]
                    out.append(sums[q] + terms[0])
                return tuple(out)

            sums = lax.fori_loop(
                0, rows // high, row, tuple(jnp.zeros((8, LANES), F32) for _ in range(group))
            )
            gram = gloc[...]
            for q in range(group):
                other = g * group + q
                total = jnp.sum(jnp.sum(sums[q], axis=1, keepdims=True), axis=0, keepdims=True)
                here = ((sub == r) & (lane == other)) | ((sub == other) & (lane == r))
                gram = gram + jnp.where(here, total, 0.0)
            gloc[...] = gram
            return carry

        lax.fori_loop(0, R // group, dots, 0)

    def step(j, carry):
        zz = nearest(j)

        @pl.when((j >= lead - 1) & (j < Z - 1))
        def _():
            pass_cotangent(j + 1)
            t3_start(j + 1)

        pl.when(j == max(Z - 2, 0))(n2_start)
        if Z > 1:
            pl.when(j == Z)(lambda: n3_start(Z - 1))

        @pl.when(j < Z)
        def _():
            r = at(zz, x)
            for o in range(X):
                turn(at(zz, other_x(o)))

            def one(h, inner):
                process(r, h)
                return inner

            lax.fori_loop(0, parts, one, 0)

        @pl.when(j >= 1)
        def _():
            for o in range(1, X):
                r = at(nearest(j - 1), other_x(o))

                def one(h, inner):
                    arrived(cbuf.at[r, h], c_rs.at[r, h])
                    process(r, h)
                    return inner

                lax.fori_loop(0, parts, one, 0)

        return carry

    lax.fori_loop(0, Z + 1, step, 0)

    def gm(o):
        return remote(gmp.at[m], gmp.at[m], gm_s.at[o], gm_r.at[o], me, other_m(o))

    def gr(o):
        return remote(grep.at[me], grep.at[me], gr_s.at[o], gr_r.at[o], other_r(o), m)

    gmp[m] = gloc[...]
    for o in range(1, M):
        gm(o).start()
    for i in range(Z - 2, 0, -1):
        n3_start(i)
    for o in range(1, M):
        gm(o).wait_recv()
    total = gmp[0]
    for o in range(1, M):
        total = total + gmp[o]
    grep[me] = total
    for o in range(1, R):
        gr(o).start()
    for o in range(1, R):
        gr(o).wait_recv()
    gram = grep[0]
    for o in range(1, R):
        gram = gram + grep[o]

    sub = lax.broadcasted_iota(jnp.int32, (grows, LANES), 0)
    lane = lax.broadcasted_iota(jnp.int32, (grows, LANES), 1)
    lane1 = lax.broadcasted_iota(jnp.int32, (1, LANES), 1)
    coef = jnp.ones((1, LANES), F32)
    count = R
    while count > 1:
        half = count // 2
        inside = (sub < count) & (lane < count)
        gram = jnp.where(inside, gram, 0.0)
        diagonal = jnp.where(sub == lane, gram, 0.0)
        crossed = jnp.where((sub == lane + half) | (lane == sub + half), gram, 0.0)
        factors = []
        for axis in (0, 1):
            square = jnp.sum(diagonal, axis=axis, keepdims=True)
            cross = jnp.sum(crossed, axis=axis, keepdims=True)
            factors.append(1.0 - cross / (2.0 * square + eps))
        scaled = jnp.where(inside, factors[0] * gram * factors[1], 0.0)
        scaled = scaled + pltpu.roll(scaled, LANES - half, 1)
        gram = scaled + pltpu.roll(scaled, grows - half, 0)
        along = jnp.broadcast_to(jnp.where(lane1 < count, factors[0], 0.0), (8, LANES))
        reach = count
        while reach < R:
            along = along + pltpu.roll(along, reach, 1)
            reach *= 2
        coef = coef * along[:1]
        count = half
    weights = [
        jnp.sum(jnp.where(lane1 == r, coef, 0.0), axis=1, keepdims=True) for r in range(R)
    ]

    own[1].wait()
    tall = min(64, rows)

    def w_rows(xx):
        return aligned(xx, rows)

    def w_across(b, o):
        piece = wbuf.at[w_rows(x), aligned(b, width)]
        return remote(piece, piece, w_s.at[b, o], w_r.at[b, x], at(z, other_x(o)), m)

    def update(b, carry):
        at_cols = aligned(b, width)

        def row(i, inner):
            at_rows = aligned(i, tall)
            total = weights[0] * grads[0, at_rows, at_cols]
            for r in range(1, R):
                total = total + weights[r] * grads[r, at_rows, at_cols]
            new = wown[at_rows, at_cols].astype(F32) - learning_rate * total
            wbuf[pl.ds(pl.multiple_of(x * rows + i * tall, tall), tall), at_cols] = new.astype(
                BF16
            )
            return inner

        lax.fori_loop(0, rows // tall, row, 0)
        for o in range(1, X):
            w_across(b, o).start()
        return carry

    lax.fori_loop(0, blocks, update, 0)
    w_out = pltpu.make_async_copy(wbuf.at[w_rows(x), :], wo_hbm, local_sem.at[3])
    w_out.start()

    def r_send(dest, b):
        to = jnp.where(dest > z, z + 1, z - 1)
        slot = jnp.where((to == dest) & (dest < z), Z, dest)
        at_cols = aligned(b, width)
        return remote(
            rsend.at[dest, :, at_cols],
            rrecv.at[slot, :, at_cols],
            rs_s.at[dest, b],
            rs_r.at[slot, b],
            at(to, x),
            m,
        )

    def r_wait(slot, b):
        piece = rrecv.at[slot, :, aligned(b, width)]
        arrived(piece, rs_r.at[slot, b])

    scale = cols * M

    def product(dest, b):
        return jnp.dot(nbuf[dest], wbuf[:, aligned(b, width)], preferred_element_type=F32)

    def pass_on(dest, b):
        at_cols = aligned(b, width)
        before = jnp.where(dest > z, z - 1, z + 1)
        more = (before >= 0) & (before < Z)
        part[...] = product(dest, b)

        @pl.when(more)
        def _():
            r_wait(dest, b)
            rsend[dest, :, at_cols] = (part[...] + rrecv[dest, :, at_cols].astype(F32)).astype(
                BF16
            )

        @pl.when(jnp.logical_not(more))
        def _():
            rsend[dest, :, at_cols] = part[...].astype(BF16)

        r_send(dest, b).start()

    def far(b, carry):
        for o in range(1, X):
            xx = other_x(o)
            arrived(wbuf.at[w_rows(xx), aligned(b, width)], w_r.at[b, xx])

        def one(i, inner):
            dest = nearest(Z - 1 - i)
            wanted = jnp.abs(dest - z) >= 2
            pl.when(wanted & (b == 0))(lambda: n3_wait(dest, n3_r))
            pl.when(wanted)(lambda: pass_on(dest, b))
            return inner

        return lax.fori_loop(0, Z - 1, one, carry)

    def near(b, carry):
        def one(i, inner):
            dest = nearest(Z - 1 - i)
            wanted = jnp.abs(dest - z) == 1
            pl.when(wanted & (b == 0))(lambda: n3_wait(dest, n3_r))
            pl.when(wanted)(lambda: pass_on(dest, b))
            return inner

        return lax.fori_loop(0, Z - 1, one, carry)

    def stay(b, carry):
        qsum[:, aligned(b, width)] = product(z, b)
        return carry

    def finish(b, carry):
        at_cols = aligned(b, width)

        @pl.when(z > 0)
        def _():
            r_wait(z, b)
            qsum[:, at_cols] = qsum[:, at_cols] + rrecv[z, :, at_cols].astype(F32)

        @pl.when(z < Z - 1)
        def _():
            r_wait(Z, b)
            qsum[:, at_cols] = qsum[:, at_cols] + rrecv[Z, :, at_cols].astype(F32)

        qbuf[:, at_cols] = (qsum[:, at_cols] * scale**-0.5).astype(BF16)
        return carry

    lax.fori_loop(0, blocks, far, 0)
    lax.fori_loop(0, blocks, near, 0)
    own[0].wait()
    lax.fori_loop(0, blocks, stay, 0)
    lax.fori_loop(0, blocks, finish, 0)
    q_out = pltpu.make_async_copy(qbuf, q_hbm, local_sem.at[4])
    q_out.start()

    for h in range(parts):
        pl.when(z < Z - 1)(lambda h=h: c_up(h).wait_send())
        pl.when(z > 0)(lambda h=h: c_down(h).wait_send())
        for j in range(Z):
            for o in range(1, X):
                c_across(j, h, o).wait_send()
        for j in range(1, Z):
            ok, copy = c_forward(j, h)
            pl.when(ok)(lambda copy=copy: copy().wait_send())
    for j in range(Z):
        for o in range(1 if j == 0 else 0, X):
            t2(j, o).wait_send()
    for o in range(1, M):
        gm(o).wait_send()
    for o in range(1, R):
        gr(o).wait_send()
    for o in range(1, M):
        t1(o).wait_send()
    for r in range(R):
        t3_wait(r, t3_s)
    for i in range(1, Z):
        n2(i).wait_send()
        n3_wait(nearest(i), n3_s)
    for b in range(blocks):
        for o in range(1, X):
            w_across(b, o).wait_send()
        for i in range(1, Z):
            r_send(nearest(i), b).wait_send()
    w_out.wait()
    q_out.wait()


def local(weight, tokens, cotangent, next_tokens):
    R = lax.axis_size("rep")
    M = lax.axis_size("mp")
    X = x_size(R)
    Z = R // X
    tok, cols = cotangent.shape
    rows = weight.shape[0]
    ntok = next_tokens.shape[0]
    width = min(256, cols)
    parts = 2 if cols % (2 * LANES) == 0 else 1
    blocks = cols // width
    grows = max(8, R)
    dma = pltpu.SemaphoreType.DMA
    anywhere = pl.BlockSpec(memory_space=pl.ANY)
    return pl.pallas_call(
        functools.partial(kernel, (Z, X, M, width)),
        out_shape=(
            jax.ShapeDtypeStruct((rows, cols), BF16),
            jax.ShapeDtypeStruct((ntok, cols), BF16),
        ),
        in_specs=[anywhere] * 4,
        out_specs=(anywhere, anywhere),
        scratch_shapes=[
            pltpu.VMEM((R, parts, tok, cols // parts), BF16),
            pltpu.VMEM((tok // M, M * cols), BF16),
            pltpu.VMEM((R, tok, rows), BF16),
            pltpu.VMEM((R, rows, tok), BF16),
            pltpu.VMEM((Z, ntok, X * rows), BF16),
            pltpu.VMEM((R, rows, cols), F32),
            pltpu.VMEM((grows, LANES), F32),
            pltpu.VMEM((M, grows, LANES), F32),
            pltpu.VMEM((R, grows, LANES), F32),
            pltpu.VMEM((rows, cols), BF16),
            pltpu.VMEM((X * rows, cols), BF16),
            pltpu.VMEM((ntok, width), F32),
            pltpu.VMEM((ntok, cols), F32),
            pltpu.VMEM((Z, ntok, cols), BF16),
            pltpu.VMEM((Z + 1, ntok, cols), BF16),
            pltpu.VMEM((ntok, cols), BF16),
            dma((5 + parts,)),
            dma((2, parts)),
            dma((Z, parts)),
            dma((Z, parts, X)),
            dma((R, parts)),
            dma((M,)),
            dma((M,)),
            dma((R,)),
            dma((R,)),
            dma((R,)),
            dma((R,)),
            dma((Z,)),
            dma((Z,)),
            dma((Z,)),
            dma((Z,)),
            dma((M,)),
            dma((M,)),
            dma((R,)),
            dma((R,)),
            dma((blocks, X)),
            dma((blocks, X)),
            dma((Z, blocks)),
            dma((Z + 1, blocks)),
        ],
        compiler_params=pltpu.CompilerParams(
            collective_id=0, has_side_effects=True, vmem_limit_bytes=60 * 1024 * 1024
        ),
    )(weight, tokens, cotangent, next_tokens)


def solution(mesh):
    in_specs = (P("rep", "mp"), P("rep", "mp"), P("rep", "mp"), P("rep", None))
    out_specs = (P("rep", "mp"), P("rep", "mp"))
    return jax.shard_map(local, mesh=mesh, in_specs=in_specs, out_specs=out_specs, check_vma=False)
```

time: 161 us -> 128 us (0.80)
  Pallas kernels: 157 us -> 123 us
    pallas_call x1, Pallas kernels: 157 us -> 123 us  [local(): pl.pallas_call(functools.partial(kernel, (Z, X, M, width)), out_shape=(ja...]
where the time goes in v2:
time: 128 us; the launch traced here: 127 us
  Pallas kernels  123 us (96%)
  local copies, waits for them, and re-layouts  3.12 us (2%)
    pallas_call x1, Pallas kernels, local(): pl.pallas_call(functools.partial(kernel, (Z, X, M, width)), out_shape=(ja...  123 us
    unnamed x4, local copies, waits for them, and re-layouts  3.12 us

profile of v2, /device:TPU:0, one launch (start us, length us, event | category | flops | bytes accessed | tf_op | source)
XLA Modules:
  0.0 127.0 jit_solution(14414868902462024085)
XLA Ops:
  0.6 123.2 %shard_map.59 = (bf16[512,1024]{1,0:T(8,128)(2,1)}, bf16[256,1024]{1,0:T(8,128)(2,1)}) custom-call(bf16[512,1024]{1,0:T(8,128)(2,1)} %w_hbm.1, bf16[256,1024]{1,0:T(8,128)(2,1)} %t_hbm.1, bf16[256,1024]{1,0:T(8,128)(2,1)} %c_hbm.1, bf16[256,4096]{1,0:T(8,128)(2,1)} %n_hbm.1), custom_call_target="tpu_custom_call" | custom-call | tf_op jit(solution)/shard_map/pallas_call | solution.py:607
  123.8 0.0 copy-start
  123.8 2.3 %copy.8 = bf16[512,1024]{1,0:T(8,128)(2,1)} copy(bf16[512,1024]{1,0:T(8,128)(2,1)} %get-tuple-element.4) | data formatting | bytes 2097152
  126.2 0.0 copy-done
  126.2 0.8 copy.9
Async XLA Ops:
  123.8 2.3 %copy-start = (bf16[256,1024]{1,0:T(8,128)(2,1)S(1)}, bf16[256,1024]{1,0:T(8,128)(2,1)}, u32[]{:S(2)}) copy-start(bf16[256,1024]{1,0:T(8,128)(2,1)} %get-tuple-element.5) | copy-start | bytes 1572868

commit v3 on v2

--- a/solution.py
+++ b/solution.py
@@ -65,6 +65,8 @@
     n2_r,
     n3_s,
     n3_r,
+    n4_s,
+    n4_r,
     gm_s,
     gm_r,
     gr_s,
@@ -119,6 +121,17 @@
     def other_m(o):
         return lax.rem(m + o, M)
 
+    ys = M // 2
+    y = m // 2
+    core = lax.rem(m, 2)
+    partner = y * 2 + 1 - core
+
+    def other_y(i):
+        return lax.rem(y + i, ys) * 2 + core
+
+    def from_y(i):
+        return lax.rem(y + ys - i, ys) * 2 + core
+
     def other_r(o):
         return lax.rem(me + o, R)
 
@@ -249,10 +262,15 @@
             for o in range(1, X):
                 c_across(j, h, o).start()
 
-    lead = min(2, Z)
-    for j in range(lead):
-        if j > 0:
-            pass_cotangent(j)
+    def pass_from(distance):
+        def one(j, carry):
+            pl.when(jnp.abs(nearest(j) - z) == distance)(lambda: pass_cotangent(j))
+            return carry
+
+        lax.fori_loop(1, Z, one, 0)
+
+    pass_from(1)
+    for j in range(min(2, Z)):
         t3_start(j)
 
     def n2(i):
@@ -266,9 +284,16 @@
             m,
         )
 
-    def n3(zz, o):
-        here = nbuf.at[zz, aligned(m, nq), :]
-        return remote(here, here, n3_s.at[zz], n3_r.at[zz], me, other_m(o))
+    def quarter(zz, q):
+        return nbuf.at[zz, aligned(q, nq), :]
+
+    def n3_y(zz, i):
+        here = quarter(zz, m)
+        return remote(here, here, n3_s.at[zz, i], n3_r.at[zz, i], me, other_y(i))
+
+    def n3_core(zz, i):
+        here = quarter(zz, m if i == 0 else from_y(i))
+        return remote(here, here, n4_s.at[zz, i], n4_r.at[zz, i], me, partner)
 
     def n2_start():
         for i in range(Z - 1, 0, -1):
@@ -278,11 +303,18 @@
         zz = nearest(i)
         here = nbuf.at[zz, aligned(m, nq), :]
         arrived(here, n2_r.at[zz])
-        for p in range(1, M):
-            n3(zz, p).start()
-
-    def n3_wait(zz, sem):
-        arrived(nbuf.at[zz, pl.ds(0, (M - 1) * nq), :], sem.at[zz])
+        for i in range(1, ys):
+            n3_y(zz, i).start()
+        n3_core(zz, 0).start()
+
+    def n3_relay(zz):
+        for i in range(1, ys):
+            arrived(quarter(zz, m), n3_r.at[zz, i])
+            n3_core(zz, i).start()
+
+    def n3_wait(zz):
+        for i in range(ys):
+            arrived(quarter(zz, m), n4_r.at[zz, i])
 
     def turn(r):
         t3_wait(r, t3_r)
@@ -340,14 +372,13 @@
     def step(j, carry):
         zz = nearest(j)
 
-        @pl.when((j >= lead - 1) & (j < Z - 1))
+        @pl.when((j >= 1) & (j < Z - 1))
         def _():
-            pass_cotangent(j + 1)
-            t3_start(j + 1)
-
-        pl.when(j == max(Z - 2, 0))(n2_start)
-        if Z > 1:
-            pl.when(j == Z)(lambda: n3_start(Z - 1))
+            pass_from(j + 1)
+
+        pl.when((j == 1) & (Z > 2))(lambda: t3_start(2))
+        pl.when((j >= 1) & (j < Z - 2))(lambda: t3_start(j + 2))
+        pl.when(j == max(Z - 1, 0))(n2_start)
 
         @pl.when(j < Z)
         def _():
@@ -386,7 +417,7 @@
     gmp[m] = gloc[...]
     for o in range(1, M):
         gm(o).start()
-    for i in range(Z - 2, 0, -1):
+    for i in range(Z - 1, 0, -1):
         n3_start(i)
     for o in range(1, M):
         gm(o).wait_recv()
@@ -514,7 +545,7 @@
         def one(i, inner):
             dest = nearest(Z - 1 - i)
             wanted = jnp.abs(dest - z) >= 2
-            pl.when(wanted & (b == 0))(lambda: n3_wait(dest, n3_r))
+            pl.when(wanted & (b == 0))(lambda: n3_wait(dest))
             pl.when(wanted)(lambda: pass_on(dest, b))
             return inner
 
@@ -524,7 +555,7 @@
         def one(i, inner):
             dest = nearest(Z - 1 - i)
             wanted = jnp.abs(dest - z) == 1
-            pl.when(wanted & (b == 0))(lambda: n3_wait(dest, n3_r))
+            pl.when(wanted & (b == 0))(lambda: n3_wait(dest))
             pl.when(wanted)(lambda: pass_on(dest, b))
             return inner
 
@@ -550,6 +581,8 @@
         qbuf[:, at_cols] = (qsum[:, at_cols] * scale**-0.5).astype(BF16)
         return carry
 
+    for i in range(Z - 1, 0, -1):
+        n3_relay(nearest(i))
     lax.fori_loop(0, blocks, far, 0)
     lax.fori_loop(0, blocks, near, 0)
     own[0].wait()
@@ -580,7 +613,11 @@
         t3_wait(r, t3_s)
     for i in range(1, Z):
         n2(i).wait_send()
-        n3_wait(nearest(i), n3_s)
+        zz = nearest(i)
+        for k in range(ys):
+            if k > 0:
+                n3_y(zz, k).wait_send()
+            n3_core(zz, k).wait_send()
     for b in range(blocks):
         for o in range(1, X):
             w_across(b, o).wait_send()
@@ -598,7 +635,7 @@
     tok, cols = cotangent.shape
     rows = weight.shape[0]
     ntok = next_tokens.shape[0]
-    width = min(256, cols)
+    width = min(128, cols)
     parts = 2 if cols % (2 * LANES) == 0 else 1
     blocks = cols // width
     grows = max(8, R)
@@ -642,8 +679,10 @@
             dma((R,)),
             dma((Z,)),
             dma((Z,)),
-            dma((Z,)),
-            dma((Z,)),
+            dma((Z, M // 2)),
+            dma((Z, M // 2)),
+            dma((Z, M // 2)),
+            dma((Z, M // 2)),
             dma((M,)),
             dma((M,)),
             dma((R,)),

time: 128 us -> 120 us (0.938)
  Pallas kernels: 123 us -> 116 us
    pallas_call x1, Pallas kernels: 123 us -> 116 us  [local(): pl.pallas_call(functools.partial(kernel, (Z, X, M, width)), out_shape=(ja...]
where the time goes in v3:
time: 120 us
  Pallas kernels  116 us (97%)
  local copies, waits for them, and re-layouts  3.12 us (3%)
    pallas_call x1, Pallas kernels, local(): pl.pallas_call(functools.partial(kernel, (Z, X, M, width)), out_shape=(ja...  116 us
    unnamed x4, local copies, waits for them, and re-layouts  3.12 us

profile of v3, /device:TPU:0, one launch (start us, length us, event | category | flops | bytes accessed | tf_op | source)
XLA Modules:
  0.0 119.5 jit_solution(11581248726956503848)
XLA Ops:
  0.6 115.7 %shard_map.59 = (bf16[512,1024]{1,0:T(8,128)(2,1)}, bf16[256,1024]{1,0:T(8,128)(2,1)}) custom-call(bf16[512,1024]{1,0:T(8,128)(2,1)} %w_hbm.1, bf16[256,1024]{1,0:T(8,128)(2,1)} %t_hbm.1, bf16[256,1024]{1,0:T(8,128)(2,1)} %c_hbm.1, bf16[256,4096]{1,0:T(8,128)(2,1)} %n_hbm.1), custom_call_target="tpu_custom_call" | custom-call | tf_op jit(solution)/shard_map/pallas_call | solution.py:644
  116.4 0.0 copy-start
  116.4 2.3 %copy.8 = bf16[512,1024]{1,0:T(8,128)(2,1)} copy(bf16[512,1024]{1,0:T(8,128)(2,1)} %get-tuple-element.4) | data formatting | bytes 2097152
  118.7 0.0 copy-done
  118.7 0.8 copy.9
Async XLA Ops:
  116.4 2.3 %copy-start = (bf16[256,1024]{1,0:T(8,128)(2,1)S(1)}, bf16[256,1024]{1,0:T(8,128)(2,1)}, u32[]{:S(2)}) copy-start(bf16[256,1024]{1,0:T(8,128)(2,1)} %get-tuple-element.5) | copy-start | bytes 1572868

commit v4 on v3

--- a/solution.py
+++ b/solution.py
@@ -417,7 +417,7 @@
     gmp[m] = gloc[...]
     for o in range(1, M):
         gm(o).start()
-    for i in range(Z - 1, 0, -1):
+    for i in range(Z - 1, 1, -1):
         n3_start(i)
     for o in range(1, M):
         gm(o).wait_recv()
@@ -427,6 +427,8 @@
     grep[me] = total
     for o in range(1, R):
         gr(o).start()
+    if Z > 1:
+        n3_start(1)
     for o in range(1, R):
         gr(o).wait_recv()
     gram = grep[0]
@@ -541,6 +543,8 @@
         for o in range(1, X):
             xx = other_x(o)
             arrived(wbuf.at[w_rows(xx), aligned(b, width)], w_r.at[b, xx])
+        if Z > 1:
+            pl.when(b == blocks // 2)(lambda: n3_relay(nearest(1)))
 
         def one(i, inner):
             dest = nearest(Z - 1 - i)
@@ -581,7 +585,7 @@
         qbuf[:, at_cols] = (qsum[:, at_cols] * scale**-0.5).astype(BF16)
         return carry
 
-    for i in range(Z - 1, 0, -1):
+    for i in range(Z - 1, 1, -1):
         n3_relay(nearest(i))
     lax.fori_loop(0, blocks, far, 0)
     lax.fori_loop(0, blocks, near, 0)
@@ -627,6 +631,27 @@
     q_out.wait()
 
 
+def settle(pieces, w_in, q_in, w_out, q_out, w_held, q_held, sems):
+    moves = []
+    for src, held, dst, base in ((w_in, w_held, w_out, 0), (q_in, q_held, q_out, pieces)):
+        tall = src.shape[0] // pieces
+        for i in range(pieces):
+            at_rows = pl.ds(i * tall, tall)
+            moves.append(
+                (
+                    pltpu.make_async_copy(src.at[at_rows], held.at[at_rows], sems.at[0, base + i]),
+                    pltpu.make_async_copy(held.at[at_rows], dst.at[at_rows], sems.at[1, base + i]),
+                )
+            )
+    for get, _ in moves:
+        get.start()
+    for get, put in moves:
+        get.wait()
+        put.start()
+    for _, put in moves:
+        put.wait()
+
+
 def local(weight, tokens, cotangent, next_tokens):
     R = lax.axis_size("rep")
     M = lax.axis_size("mp")
@@ -641,7 +666,7 @@
     grows = max(8, R)
     dma = pltpu.SemaphoreType.DMA
     anywhere = pl.BlockSpec(memory_space=pl.ANY)
-    return pl.pallas_call(
+    results = pl.pallas_call(
         functools.partial(kernel, (Z, X, M, width)),
         out_shape=(
             jax.ShapeDtypeStruct((rows, cols), BF16),
@@ -696,6 +721,21 @@
             collective_id=0, has_side_effects=True, vmem_limit_bytes=60 * 1024 * 1024
         ),
     )(weight, tokens, cotangent, next_tokens)
+    pieces = 4
+    return pl.pallas_call(
+        functools.partial(settle, pieces),
+        out_shape=(
+            jax.ShapeDtypeStruct((rows, cols), BF16),
+            jax.ShapeDtypeStruct((ntok, cols), BF16),
+        ),
+        in_specs=[anywhere] * 2,
+        out_specs=(anywhere, anywhere),
+        scratch_shapes=[
+            pltpu.VMEM((rows, cols), BF16),
+            pltpu.VMEM((ntok, cols), BF16),
+            dma((2, 2 * pieces)),
+        ],
+    )(*results)
 
 
 def solution(mesh):

time: 120 us -> 118 us (0.983)
  local copies, waits for them, and re-layouts: 3.12 us -> 0 us
  Pallas kernels: 116 us -> 118 us
    unnamed x4 -> x0, local copies, waits for them, and re-layouts: 3.12 us -> none
    pallas_call x0 -> x1, Pallas kernels: none -> 2.22 us  [local(): pl.pallas_call(functools.partial(settle, pieces), out_shape=(jax.ShapeDty...]
where the time goes in v4:
time: 118 us
  Pallas kernels  118 us (100%)
    pallas_call x1, Pallas kernels, local(): pl.pallas_call(functools.partial(kernel, (Z, X, M, width)), out_shape=(ja...  115 us

profile of v4, /device:TPU:0, one launch (start us, length us, event | category | flops | bytes accessed | tf_op | source)
XLA Modules:
  0.0 118.2 jit_solution(4490850420232370946)
XLA Ops:
  0.6 115.3 %shard_map.59 = (bf16[512,1024]{1,0:T(8,128)(2,1)}, bf16[256,1024]{1,0:T(8,128)(2,1)}) custom-call(bf16[512,1024]{1,0:T(8,128)(2,1)} %w_hbm.1, bf16[256,1024]{1,0:T(8,128)(2,1)} %t_hbm.1, bf16[256,1024]{1,0:T(8,128)(2,1)} %c_hbm.1, bf16[256,4096]{1,0:T(8,128)(2,1)} %n_hbm.1), custom_call_target="tpu_custom_call" | custom-call | tf_op jit(solution)/shard_map/pallas_call | solution.py:669
  116.0 2.2 %shard_map.60 = (bf16[512,1024]{1,0:T(8,128)(2,1)}, bf16[256,1024]{1,0:T(8,128)(2,1)}) custom-call(bf16[512,1024]{1,0:T(8,128)(2,1)} %get-tuple-element.4.w_in, bf16[256,1024]{1,0:T(8,128)(2,1)} %get-tuple-element.5.q_in), custom_call_target="tpu_custom_call" | custom-call | tf_op jit(solution)/shard_map/pallas_call | solution.py:725

commit v5 on v4

--- a/solution.py
+++ b/solution.py
@@ -380,6 +380,18 @@
         pl.when((j >= 1) & (j < Z - 2))(lambda: t3_start(j + 2))
         pl.when(j == max(Z - 1, 0))(n2_start)
 
+        @pl.when(j >= 1)
+        def _():
+            for o in range(1, X):
+                r = at(nearest(j - 1), other_x(o))
+
+                def one(h, inner):
+                    arrived(cbuf.at[r, h], c_rs.at[r, h])
+                    process(r, h)
+                    return inner
+
+                lax.fori_loop(0, parts, one, 0)
+
         @pl.when(j < Z)
         def _():
             r = at(zz, x)
@@ -391,18 +403,6 @@
                 return inner
 
             lax.fori_loop(0, parts, one, 0)
-
-        @pl.when(j >= 1)
-        def _():
-            for o in range(1, X):
-                r = at(nearest(j - 1), other_x(o))
-
-                def one(h, inner):
-                    arrived(cbuf.at[r, h], c_rs.at[r, h])
-                    process(r, h)
-                    return inner
-
-                lax.fori_loop(0, parts, one, 0)
 
         return carry
 

time: 118 us -> 117 us (level)
  Pallas kernels: 118 us -> 116 us
    pallas_call x1, Pallas kernels: 115 us -> 114 us  [local(): pl.pallas_call(functools.partial(kernel, (Z, X, M, width)), out_shape=(ja...]
where the time goes in v5:
time: 117 us
  Pallas kernels  116 us (99%)
    pallas_call x1, Pallas kernels, local(): pl.pallas_call(functools.partial(kernel, (Z, X, M, width)), out_shape=(ja...  114 us

profile of v5, /device:TPU:0, one launch (start us, length us, event | category | flops | bytes accessed | tf_op | source)
XLA Modules:
  0.0 116.7 jit_solution(613002724354386784)
XLA Ops:
  0.6 113.8 %shard_map.59 = (bf16[512,1024]{1,0:T(8,128)(2,1)}, bf16[256,1024]{1,0:T(8,128)(2,1)}) custom-call(bf16[512,1024]{1,0:T(8,128)(2,1)} %w_hbm.1, bf16[256,1024]{1,0:T(8,128)(2,1)} %t_hbm.1, bf16[256,1024]{1,0:T(8,128)(2,1)} %c_hbm.1, bf16[256,4096]{1,0:T(8,128)(2,1)} %n_hbm.1), custom_call_target="tpu_custom_call" | custom-call | tf_op jit(solution)/shard_map/pallas_call | solution.py:669
  114.4 2.2 %shard_map.60 = (bf16[512,1024]{1,0:T(8,128)(2,1)}, bf16[256,1024]{1,0:T(8,128)(2,1)}) custom-call(bf16[512,1024]{1,0:T(8,128)(2,1)} %get-tuple-element.4.w_in, bf16[256,1024]{1,0:T(8,128)(2,1)} %get-tuple-element.5.q_in), custom_call_target="tpu_custom_call" | custom-call | tf_op jit(solution)/shard_map/pallas_call | solution.py:725
